TPU v7x, 32 devices: a whole 2x2x4 slice. The times are simulated.
32 devices in a mesh: sec: 2 (over core), blk: 8 (over z, x), ch: 2 (over y).
Axes of the slice: x: 2, y: 2, z: 4, core: 2. Of those that a mesh axis runs over, the one named last changes fastest.
Arguments:
- voltages: bfloat16 [123, 4096, 2048], P(None, 'blk', ('sec', 'ch')), may hold values from -6 to 6
Outputs:
- visibilities: bfloat16 [16, 2, 4096, 4096], P(('sec', 'ch'), None, 'blk')
All inputs are finite; a program needn't handle non-finite values.
Results may differ from a plain program's by a relative error of at most 0.0082.
Values may be sent and summed in bfloat16 or wider, within the bound.
A program may use at most 384 MiB of HBM per device.

v0:
```python
import math
import jax
import jax.numpy as jnp
from jax import lax
from jax.sharding import PartitionSpec as P

FFT = 2048
TAPS = 4
CH_GRP = 4


def make_window(tap_count, frame_len):
    position = jnp.arange(tap_count * frame_len, dtype=jnp.float32)
    offset = (position - tap_count * frame_len / 2 + 0.5) / frame_len
    taper = 0.5 - 0.5 * jnp.cos(2.0 * jnp.pi * (position + 0.5) / (tap_count * frame_len))
    profile = jnp.sinc(offset) * taper
    profile = profile * jnp.sqrt(frame_len / jnp.sum(profile * profile))
    return profile.reshape(tap_count, frame_len)


def dft_table(frame_len, chan_count, bank_size):
    spacing = bank_size // chan_count
    chosen = jnp.arange(chan_count, dtype=jnp.int32) * spacing + spacing // 2
    phases = jnp.arange(frame_len, dtype=jnp.int32)[:, None] * chosen[None, :] % frame_len
    angles = 2.0 * jnp.pi / frame_len * phases.astype(jnp.float32)
    factor = 1.0 / math.sqrt(frame_len)
    weights = jnp.stack([jnp.cos(angles) * factor, -jnp.sin(angles) * factor], axis=-1)
    return weights.reshape(frame_len, chan_count * 2).astype(jnp.bfloat16)


def pair_block(local_panel, remote_panel, steps):
    grams = jnp.einsum(
        "crti,cqtj->crqij", local_panel, remote_panel, preferred_element_type=jnp.float32
    )
    real_sum = grams[:, 0, 0] + grams[:, 1, 1]
    imag_sum = grams[:, 1, 0] - grams[:, 0, 1]
    return jnp.stack([real_sum, imag_sum], axis=1) / steps


def body(voltages):
    groups = lax.axis_size("sec") * lax.axis_size("ch")
    span_len = voltages.shape[2]
    panel_len = voltages.shape[1]
    steps = voltages.shape[0] - TAPS + 1
    chan_total = CH_GRP * groups
    group_pos = lax.axis_index("sec") * lax.axis_size("ch") + lax.axis_index("ch")
    first = group_pos * span_len
    window = lax.dynamic_slice_in_dim(make_window(TAPS, FFT), first, span_len, 1)
    summed = jnp.zeros((steps, panel_len, span_len), jnp.float32)
    for tap_index in range(TAPS):
        summed = summed + window[tap_index] * voltages[tap_index : tap_index + steps].astype(
            jnp.float32
        )
    filtered = summed.astype(jnp.bfloat16)
    weights = lax.dynamic_slice_in_dim(dft_table(FFT, chan_total, FFT // 2), first, span_len, 0)
    terms = jnp.einsum("tsn,nk->kts", filtered, weights, preferred_element_type=jnp.float32)
    spectra = lax.psum_scatter(
        terms.reshape(CH_GRP * lax.axis_size(("sec", "ch")), 2, steps, panel_len),
        ("sec", "ch"),
        scatter_dimension=0,
        tiled=True,
    ).astype(jnp.bfloat16)
    block = pair_block(spectra, lax.all_gather(spectra, "blk", axis=3, tiled=True), steps)
    return block.astype(jnp.bfloat16)


def solution(mesh):
    return jax.shard_map(
        body,
        mesh=mesh,
        in_specs=(P(None, "blk", ("sec", "ch")),),
        out_specs=P(("sec", "ch"), None, "blk", None),
        check_vma=False,
    )
```

profile of v0, /device:TPU:0, one launch (start us, length us, event | category | flops | bytes accessed | tf_op | source)
XLA Modules:
  0.0 491.0 jit_solution(1568423521587529917)
XLA Ops:
  6.5 0.0 reduce-scatter.2.cloned.1.call-start
  6.5 0.8 fusion.49
  7.4 0.1 select_select_fusion
  7.5 0.1 multiply_add_fusion.1
  8.3 0.1 fusion.52
  8.4 0.6 multiply_convert_fusion.1
  9.0 0.1 copy.10
  9.2 0.1 convert_element_type.47
  9.2 82.8 %fusion.1 = f32[32,120,512]{2,0,1:T(8,128)} fusion(bf16[123,512,512]{2,1,0:T(8,128)(2,1)} %param.1, f32[512]{0:T(512)S(1)} %bitcast.42, f32[512]{0:T(512)S(1)} %bitcast.40, f32[512]{0:T(512)S(1)} %bitcast.41, f32[512]{0:T(512)S(1)} %bitcast.39, bf16[2048,32]{0,1:T(8,128)(2,1)S(1)} %convert_element_type.47, s32[]{:T(128)S(6)} %select_n.62), kind=kOutput, calls=%fused_computation.3 | convolution fusion | flops 2390753280 | bytes 259563520 | tf_op jit(solution)/shard_map/tsn,nk->kts/dot_general | solution.py:56
  92.0 10.9 %copy.17 = f32[32,120,512]{2,1,0:T(8,128)} copy(f32[32,120,512]{2,0,1:T(8,128)} %fusion.1) | data formatting | bytes 15728640 | tf_op jit(solution)/shard_map/reshape | solution.py:58
  102.9 0.0 reduce-scatter.2.cloned.1.call-update
  102.9 0.2 all-gather.2.cloned.1.call-start
  103.1 71.6 %reduce-scatter.2.cloned.1.call-done = f32[4,2,120,512]{3,2,1,0:T(8,128)} async-done(((f32[16,2,120,512]{3,2,1,0:T(8,128)}), f32[4,2,120,512]{3,2,1,0:T(8,128)}) %reduce-scatter.2.cloned.1.call-update) | async-done | bytes 1966096 | tf_op jit(solution)/shard_map/reduce_scatter | solution.py:57
  174.7 2.6 convert_element_type.53
  177.4 0.0 all-gather.2.cloned.1.call-update
  177.4 119.1 %all-gather.2.cloned.1.call-done = bf16[4,2,120,4096]{3,2,1,0:T(8,128)(2,1)} async-done(((bf16[4,2,120,512]{3,2,1,0:T(8,128)(2,1)}), bf16[4,2,120,4096]{3,2,1,0:T(8,128)(2,1)}) %all-gather.2.cloned.1.call-update) | async-done | bytes 7864336 | tf_op jit(solution)/shard_map/all_gather | solution.py:63
  296.5 47.8 %convolution_bitcast_fusion = f32[4,2,2,512,4096]{3,4,1,2,0:T(8,128)} fusion(bf16[4,2,120,4096]{3,2,1,0:T(8,128)(2,1)} %all-gather.2.cloned.1.call-done, bf16[4,2,120,512]{3,2,1,0:T(8,128)(2,1)} %convert_element_type.53), kind=kOutput, calls=%fused_computation.4 | convolution fusion | flops 8053063680 | bytes 143065088 | tf_op jit(solution)/shard_map/crti,cqtj->crqij/dot_general | solution.py:32
  344.3 33.2 %fusion.2 = f32[4,1,512,4096]{2,3,0,1:T(8,128)} fusion(f32[4,2,2,512,4096]{3,4,1,2,0:T(8,128)} %convolution_bitcast_fusion), kind=kLoop, calls=%fused_computation.6 | loop fusion | flops 8388608 | bytes 100663296 | tf_op jit(solution)/shard_map/sub | solution.py:36
  377.5 33.1 %fusion.4 = f32[4,1,512,4096]{2,3,0,1:T(8,128)} fusion(f32[4,2,2,512,4096]{3,4,1,2,0:T(8,128)} %convolution_bitcast_fusion), kind=kLoop, calls=%fused_computation.9 | loop fusion | flops 8388608 | bytes 100663296 | tf_op jit(solution)/shard_map/add | solution.py:35
  410.6 32.9 %fusion = bf16[4,2,512,4096]{2,3,0,1:T(8,128)(2,1)} fusion(f32[4,1,512,4096]{2,3,0,1:T(8,128)} %fusion.2, f32[4,1,512,4096]{2,3,0,1:T(8,128)} %fusion.4), kind=kLoop, calls=%fused_computation.2 | loop fusion | flops 50331648 | bytes 100663296 | tf_op jit(solution)/shard_map/convert_element_type | solution.py:64
  443.5 40.6 %copy.14 = bf16[4,2,512,4096]{3,2,1,0:T(8,128)(2,1)} copy(bf16[4,2,512,4096]{2,3,0,1:T(8,128)(2,1)} %fusion) | data formatting | bytes 67108864 | tf_op jit(solution)/shard_map/convert_element_type | solution.py:64
  (5 shorter events, 0.1 us)
Async XLA Ops:
  6.5 168.2 %reduce-scatter.2.cloned.1.call-start = ((), (), s32[]{:S(2)}) async-start(), calls=%async_computation.1 | async-start | bytes 9830400 | tf_op jit(solution)/shard_map/reduce_scatter | solution.py:57
  102.9 193.6 %all-gather.2.cloned.1.call-start = ((), (), s32[]{:S(2)}) async-start(), calls=%async_computation.2 | async-start | bytes 8847360 | tf_op jit(solution)/shard_map/all_gather | solution.py:63
Sparse Core Ops, SparseCore 0:
  103.0 71.6 reduce-scatter.1
  177.5 118.9 all-gather.1
where the time goes:
time: 492 us; the launch traced here: 491 us
  waiting for transfers between devices  191 us (39%)
  matrix products  131 us (27%)
  other arithmetic  104 us (21%)
  local copies, waits for them, and re-layouts  51.7 us (11%)
  between operations  14.2 us (3%)
    all_gather x1, waiting for transfers between devices, body(): lax.all_gather(spectra, 'blk', axis=3, tiled=True)  119 us
    dot_general x1, matrix products, body(): jnp.einsum('tsn,nk->kts', filtered, weights, preferred_element_type=jnp.f...  82.8 us
    reduce_scatter x1, waiting for transfers between devices, body(): lax.psum_scatter(terms.reshape(CH_GRP * lax.axis_size(('sec', 'ch')), 2,...  71.6 us
    dot_general x1, matrix products, pair_block(): jnp.einsum('crti,cqtj->crqij', local_panel, remote_panel, preferred_eleme...  47.8 us
    convert_element_type x1, local copies, waits for them, and re-layouts, body(): return block.astype(jnp.bfloat16)  40.6 us
    sub x1, other arithmetic, pair_block(): imag_sum = grams[:, 1, 0] - grams[:, 0, 1]  33.2 us
    add x1, other arithmetic, pair_block(): real_sum = grams[:, 0, 0] + grams[:, 1, 1]  33.1 us
    convert_element_type x1, other arithmetic, body(): return block.astype(jnp.bfloat16)  32.9 us
  transfers between devices with their start and end apart: 2, of which 2 were waited for; matrix products, arithmetic and copies ran while one was open for 0% of the time, Pallas kernels for 0%

commit v1 on v0

--- a/solution.py
+++ b/solution.py
@@ -3,10 +3,26 @@
 import jax.numpy as jnp
 from jax import lax
 from jax.sharding import PartitionSpec as P
+from jax.lax import axis_index, axis_size, ppermute
 
 FFT = 2048
 TAPS = 4
 CH_GRP = 4
+
+
+def handle_heads(mine_x, mesh_ax):
+    outer = axis_size(mesh_ax)
+    mixed_arr = axis_index(mesh_ax)
+    taken_in, top = (outer, mixed_arr)
+    val2, u1 = (mine_x, 1)
+    while u1 < taken_in:
+        work_now = tuple(((d, d ^ u1) for d in range(taken_in)))
+        v_now = ppermute(val2, mesh_ax, perm=work_now)
+        res = jnp.concatenate([val2, v_now], 3)
+        m_next = jnp.concatenate([v_now, val2], axis=3)
+        val2 = jnp.where(top & u1 == 0, res, m_next)
+        u1 = 2 * u1
+    return val2
 
 
 def make_window(tap_count, frame_len):
@@ -60,7 +76,7 @@
         scatter_dimension=0,
         tiled=True,
     ).astype(jnp.bfloat16)
-    block = pair_block(spectra, lax.all_gather(spectra, "blk", axis=3, tiled=True), steps)
+    block = pair_block(spectra, handle_heads(spectra, "blk"), steps)
     return block.astype(jnp.bfloat16)
 
 

time: 492 us -> 620 us (1.26)
  waiting for transfers between devices: 191 us -> 304 us
    ppermute x0 -> x3, waiting for transfers between devices: none -> 233 us  [handle_heads(): v_now = ppermute(val2, mesh_ax, perm=work_now)]
    all_gather x1 -> x0, waiting for transfers between devices: 119 us -> none  [body(): lax.all_gather(spectra, 'blk', axis=3, tiled=True)]
    select_n x0 -> x2, other arithmetic: none -> 7.03 us  [handle_heads(): val2 = jnp.where(top & u1 == 0, res, m_next)]
  transfers between devices with their start and end apart: 2 -> 4, of which waited for: 2 -> 4; matrix products, arithmetic and copies ran while one was open for 0% -> 0% of each run, Pallas kernels for 0% -> 0%
where the time goes in v1:
time: 620 us; the launch traced here: 619 us
  waiting for transfers between devices  304 us (49%)
  matrix products  133 us (21%)
  other arithmetic  110 us (18%)
  local copies, waits for them, and re-layouts  51.7 us (8%)
  between operations  14.2 us (2%)
    ppermute x3, waiting for transfers between devices, handle_heads(): v_now = ppermute(val2, mesh_ax, perm=work_now)  233 us
    dot_general x1, matrix products, body(): jnp.einsum('tsn,nk->kts', filtered, weights, preferred_element_type=jnp.f...  82.8 us
    reduce_scatter x1, waiting for transfers between devices, body(): lax.psum_scatter(terms.reshape(CH_GRP * lax.axis_size(('sec', 'ch')), 2,...  71.8 us
    dot_general x1, matrix products, pair_block(): jnp.einsum('crti,cqtj->crqij', local_panel, remote_panel, preferred_eleme...  50.7 us
    convert_element_type x1, local copies, waits for them, and re-layouts, body(): return block.astype(jnp.bfloat16)  40.6 us
    sub x1, other arithmetic, pair_block(): imag_sum = grams[:, 1, 0] - grams[:, 0, 1]  33.2 us
    add x1, other arithmetic, pair_block(): real_sum = grams[:, 0, 0] + grams[:, 1, 1]  33.1 us
    convert_element_type x1, other arithmetic, body(): return block.astype(jnp.bfloat16)  32.9 us
  transfers between devices with their start and end apart: 4, of which 4 were waited for; matrix products, arithmetic and copies ran while one was open for 0% of the time, Pallas kernels for 0%

profile of v1, /device:TPU:0, one launch (start us, length us, event | category | flops | bytes accessed | tf_op | source)
XLA Modules:
  0.0 618.8 jit_solution(7265574243323415943)
XLA Ops:
  6.5 0.0 reduce-scatter.2.cloned.1.call-start
  6.5 0.8 fusion.56
  7.4 0.1 select_select_fusion
  7.5 0.1 multiply_add_fusion.1
  8.3 0.1 fusion.59
  8.4 0.6 multiply_convert_fusion.1
  9.0 0.1 copy.10
  9.2 0.1 convert_element_type.47
  9.2 82.8 %fusion.1 = f32[32,120,512]{2,0,1:T(8,128)} fusion(bf16[123,512,512]{2,1,0:T(8,128)(2,1)} %param.1, f32[512]{0:T(512)S(1)} %bitcast.46, f32[512]{0:T(512)S(1)} %bitcast.44, f32[512]{0:T(512)S(1)} %bitcast.45, f32[512]{0:T(512)S(1)} %bitcast.43, bf16[2048,32]{0,1:T(8,128)(2,1)S(1)} %convert_element_type.47, s32[]{:T(128)S(6)} %select_n.89), kind=kOutput, calls=%fused_computation.3 | convolution fusion | flops 2390753280 | bytes 259563520 | tf_op jit(solution)/shard_map/tsn,nk->kts/dot_general | solution.py:72
  92.0 10.9 %copy.17 = f32[32,120,512]{2,1,0:T(8,128)} copy(f32[32,120,512]{2,0,1:T(8,128)} %fusion.1) | data formatting | bytes 15728640 | tf_op jit(solution)/shard_map/reshape | solution.py:74
  102.9 0.0 reduce-scatter.2.cloned.1.call-update
  102.9 71.8 %reduce-scatter.2.cloned.1.call-done = f32[4,2,120,512]{3,2,1,0:T(8,128)} async-done(((f32[16,2,120,512]{3,2,1,0:T(8,128)}), f32[4,2,120,512]{3,2,1,0:T(8,128)}) %reduce-scatter.2.cloned.1.call-update) | async-done | bytes 1966096 | tf_op jit(solution)/shard_map/reduce_scatter | solution.py:73
  174.7 1.7 convert_element_type.53
  176.4 1.5 collective-permute-start
  177.9 22.1 %collective-permute-done = bf16[4,2,120,512]{3,2,1,0:T(8,128)(2,1)} collective-permute-done((bf16[4,2,120,512]{3,2,1,0:T(8,128)(2,1)S(1)}, bf16[4,2,120,512]{3,2,1,0:T(8,128)(2,1)}, u32[]{:S(2)}, u32[]{:S(2)}) %collective-permute-start) | collective-permute-done | bytes 983072 | tf_op jit(solution)/shard_map/ppermute | solution.py:20
  200.1 2.2 maximum_select_fusion.2
  202.3 1.5 collective-permute-start.1
  203.8 42.3 %collective-permute-done.1 = bf16[4,2,120,1024]{3,2,1,0:T(8,128)(2,1)} collective-permute-done((bf16[4,2,120,1024]{3,2,1,0:T(8,128)(2,1)S(1)}, bf16[4,2,120,1024]{3,2,1,0:T(8,128)(2,1)}, u32[]{:S(2)}, u32[]{:S(2)}) %collective-permute-start.1) | collective-permute-done | bytes 1966112 | tf_op jit(solution)/shard_map/ppermute | solution.py:20
  246.1 4.9 maximum_select_fusion.1
  251.0 2.4 collective-permute-start.2
  253.4 168.1 %collective-permute-done.2 = bf16[4,2,120,2048]{3,2,1,0:T(8,128)(2,1)} collective-permute-done((bf16[4,2,120,2048]{3,2,1,0:T(8,128)(2,1)}, bf16[4,2,120,2048]{3,2,1,0:T(8,128)(2,1)}, u32[]{:S(2)}, u32[]{:S(2)}) %collective-permute-start.2) | collective-permute-done | bytes 3932192 | tf_op jit(solution)/shard_map/ppermute | solution.py:20
  421.4 50.7 %convolution_bitcast_fusion = f32[4,2,2,512,4096]{3,4,1,2,0:T(8,128)} fusion(bf16[4,2,120,2048]{3,2,1,0:T(8,128)(2,1)} %collective-permute-done.2, bf16[4,2,120,2048]{3,2,1,0:T(8,128)(2,1)} %maximum_select_fusion.1, pred[]{:T(512)S(6)} %eq.38, bf16[4,2,120,512]{3,2,1,0:T(8,128)(2,1)S(1)} %convert_element_type.53), kind=kOutput, calls=%fused_computation.4 | convolution fusion | flops 8088453120 | bytes 143065088 | tf_op jit(solution)/shard_map/crti,cqtj->crqij/dot_general | solution.py:48
  472.1 33.2 %fusion.2 = f32[4,1,512,4096]{2,3,0,1:T(8,128)} fusion(f32[4,2,2,512,4096]{3,4,1,2,0:T(8,128)} %convolution_bitcast_fusion), kind=kLoop, calls=%fused_computation.6 | loop fusion | flops 8388608 | bytes 100663296 | tf_op jit(solution)/shard_map/sub | solution.py:52
  505.3 33.1 %fusion.4 = f32[4,1,512,4096]{2,3,0,1:T(8,128)} fusion(f32[4,2,2,512,4096]{3,4,1,2,0:T(8,128)} %convolution_bitcast_fusion), kind=kLoop, calls=%fused_computation.9 | loop fusion | flops 8388608 | bytes 100663296 | tf_op jit(solution)/shard_map/add | solution.py:51
  538.4 32.9 %fusion = bf16[4,2,512,4096]{2,3,0,1:T(8,128)(2,1)} fusion(f32[4,1,512,4096]{2,3,0,1:T(8,128)} %fusion.2, f32[4,1,512,4096]{2,3,0,1:T(8,128)} %fusion.4), kind=kLoop, calls=%fused_computation.2 | loop fusion | flops 50331648 | bytes 100663296 | tf_op jit(solution)/shard_map/convert_element_type | solution.py:80
  571.3 40.6 %copy.14 = bf16[4,2,512,4096]{3,2,1,0:T(8,128)(2,1)} copy(bf16[4,2,512,4096]{2,3,0,1:T(8,128)(2,1)} %fusion) | data formatting | bytes 67108864 | tf_op jit(solution)/shard_map/convert_element_type | solution.py:80
  (5 shorter events, 0.1 us)
Async XLA Ops:
  6.5 168.2 %reduce-scatter.2.cloned.1.call-start = ((), (), s32[]{:S(2)}) async-start(), calls=%async_computation.1 | async-start | bytes 9830400 | tf_op jit(solution)/shard_map/reduce_scatter | solution.py:73
  176.4 23.7 %collective-permute-start = (bf16[4,2,120,512]{3,2,1,0:T(8,128)(2,1)S(1)}, bf16[4,2,120,512]{3,2,1,0:T(8,128)(2,1)}, u32[]{:S(2)}, u32[]{:S(2)}) collective-permute-start(bf16[4,2,120,512]{3,2,1,0:T(8,128)(2,1)S(1)} %convert_element_type.53), channel_id=1, source_target_pairs={{0,2},{2,0},{4,6},{6,4},{8,10},{10,8},{12,14},{14,12},{1,3},{3,1},... | collective-permute-start | bytes 2949128 | tf_op jit(solution)/shard_map/ppermute | solution.py:20
  202.3 43.9 %collective-permute-start.1 = (bf16[4,2,120,1024]{3,2,1,0:T(8,128)(2,1)S(1)}, bf16[4,2,120,1024]{3,2,1,0:T(8,128)(2,1)}, u32[]{:S(2)}, u32[]{:S(2)}) collective-permute-start(bf16[4,2,120,1024]{3,2,1,0:T(8,128)(2,1)S(1)} %maximum_select_fusion.2), channel_id=1, source_target_pairs={{0,4},{2,6},{4,0},{6,2},{8,12},{10,14},{12,8},{14,10},{1,5},{3,7},... | collective-permute-start | bytes 5898248 | tf_op jit(solution)/shard_map/ppermute | solution.py:20
  251.0 170.4 %collective-permute-start.2 = (bf16[4,2,120,2048]{3,2,1,0:T(8,128)(2,1)}, bf16[4,2,120,2048]{3,2,1,0:T(8,128)(2,1)}, u32[]{:S(2)}, u32[]{:S(2)}) collective-permute-start(bf16[4,2,120,2048]{3,2,1,0:T(8,128)(2,1)} %maximum_select_fusion.1), channel_id=1, source_target_pairs={{0,8},{2,10},{4,12},{6,14},{8,0},{10,2},{12,4},{14,6},{1,9},{3,11}... | collective-permute-start | bytes 11796488 | tf_op jit(solution)/shard_map/ppermute | solution.py:20
Sparse Core Ops, SparseCore 0:
  103.0 71.6 reduce-scatter.1
